TPU v7x, 32 devices: a whole 2x2x4 slice. The times are simulated.
32 devices in a mesh: vel: 2 (over core), sx: 4 (over y, x), sy: 4 (over z).
Axes of the slice: x: 2, y: 2, z: 4, core: 2. Of those that a mesh axis runs over, the one named last changes fastest.
Arguments:
- particle_distributions: bfloat16 [512, 32, 512], P('vel', 'sx', 'sy'), may hold values from 0.099609375 to 2
- integer_grid_displacements: int32 [2, 512], P(None, 'vel'), may hold values from -4 to 3, as said below
- leftover_shift_part: float32 [2, 512], P(None, 'vel'), may hold values from 0 to 1
- relaxing_frequency_dt: float32 [32, 512], P('sx', 'sy'), may hold values from 0.1 to 3
- solid_indicator: int32 [32, 512], P('sx', 'sy'), may hold values 0 or 1
- solid_heat_level: float32 [1], replicated, may hold values from 0.5 to 4
Outputs:
- advanced: bfloat16 [512, 32, 512], P('vel', 'sx', 'sy')
Inputs may be any that keep to these rules, and one draw needn't show every extreme that they name: `integer_grid_displacements`: row 0 grows with the velocity's index by steps of at most one, up to a random step of one; row 1 is arbitrary. Both rows reach both ends.
All inputs are finite; a program needn't handle non-finite values. No bound on the sum of `solid_indicator` on one device may be relied on, other than what follows from the above.
Results may differ from a plain program's by a relative error of at most 0.0028.
Values may be sent and summed in bfloat16 or wider, within the bound.
A program may use at most 128 MiB of HBM per device.

v0:
```python
import functools
import math

import jax
import jax.numpy as jnp
from jax import lax
from jax.experimental import pallas as pl
from jax.experimental.pallas import tpu as pltpu
from jax.sharding import PartitionSpec as P

MAXS = 4
STEPS = 2
ROWS = 8
LANES = 128
GROUP = 16
SPAN = 24
LOG2E = math.log2(math.e)
F32 = jnp.float32
BF16 = jnp.bfloat16


def kernel(
    sizes,
    disp,
    frac,
    heat,
    x_ref,
    freq_ref,
    solid_ref,
    o_ref,
    ext,
    pext,
    pack_f,
    moved_ref,
    prof_ref,
    wall_ref,
    xsend,
    psend,
    csend,
    xrecv,
    precv,
    crecv,
    msend,
    mrecv,
    zsend,
    zrecv,
    xs_sem,
    xr_sem,
    ps_sem,
    pr_sem,
    cs_sem,
    cr_sem,
    ms_sem,
    mr_sem,
    zs_sem,
    zr_sem,
):
    nvel, nsx, nsy = sizes
    nv = disp.shape[1]
    groups = nv // GROUP
    vel = lax.axis_index("vel")
    sx = lax.axis_index("sx")
    sy = lax.axis_index("sy")
    up, down = lax.rem(sx + 1, nsx), lax.rem(sx + nsx - 1, nsx)
    right, left = lax.rem(sy + 1, nsy), lax.rem(sy + nsy - 1, nsy)
    peers = [lax.rem(vel + p, nvel) for p in range(1, nvel)]
    sources = [lax.rem(vel + nvel - p, nvel) for p in range(1, nvel)]

    def at(v, i, j):
        return (v, i, j)

    spatial = [
        at(vel, up, sy), at(vel, down, sy), at(vel, sx, right), at(vel, sx, left),
        at(vel, up, right), at(vel, up, left), at(vel, down, right), at(vel, down, left),
    ]
    barrier = pltpu.get_barrier_semaphore()
    for target in spatial + [at(p, sx, sy) for p in peers]:
        pl.semaphore_signal(barrier, inc=1, device_id=target, device_id_type=pl.DeviceIdType.MESH)

    lane = lax.broadcasted_iota(jnp.int32, (ROWS, LANES), 1)
    centered = jnp.where(lane < LANES // 2, lane, lane - LANES)
    slot = lane // 8
    from_left = lax.rem(lane, 8) < 4

    def remote(src, dst, send_sem, recv_sem, target):
        return pltpu.make_async_remote_copy(
            src_ref=src, dst_ref=dst, send_sem=send_sem, recv_sem=recv_sem,
            device_id=target, device_id_type=pl.DeviceIdType.MESH,
        )

    def halo_copies(step):
        copies = [
            remote(xsend.at[step, 0], xrecv.at[step, 0], xs_sem.at[step, 0], xr_sem.at[step, 0], spatial[0]),
            remote(xsend.at[step, 1], xrecv.at[step, 1], xs_sem.at[step, 1], xr_sem.at[step, 1], spatial[1]),
            remote(psend.at[step], precv.at[step, 0], ps_sem.at[step, 0], pr_sem.at[step, 0], spatial[2]),
            remote(psend.at[step], precv.at[step, 1], ps_sem.at[step, 1], pr_sem.at[step, 1], spatial[3]),
        ]
        for c in range(4):
            copies.append(
                remote(csend.at[step, c // 2], crecv.at[step, c], cs_sem.at[step, c], cr_sem.at[step, c], spatial[4 + c])
            )
        return copies

    def stow(step, g, planes):
        packed = None
        for k, plane in enumerate(planes):
            ext[pl.ds(pl.multiple_of((g * GROUP + k) * SPAN, 8) + 8, ROWS), :] = plane
            turned = pltpu.roll(plane, (8 * k + 4) % LANES, 1)
            packed = turned if packed is None else jnp.where(slot == k, turned, packed)
        pack_f[pl.ds(pl.multiple_of(g * ROWS, 8), ROWS), :] = packed
        for q in range(GROUP // 4):
            four = planes[4 * q: 4 * q + 4]
            base = pl.multiple_of(g * (GROUP * 4) + q * 16, 16)
            xsend[step, 0, pl.ds(base, 16), :] = jnp.concatenate([f[4:8] for f in four], 0).astype(BF16)
            xsend[step, 1, pl.ds(base, 16), :] = jnp.concatenate([f[0:4] for f in four], 0).astype(BF16)

    def finish_pack(step):
        psend[step] = pack_f[...].astype(BF16)
        for j in range(groups // 4):
            for side, first in ((0, 4), (1, 0)):
                pieces = [pack_f[(4 * j + i) * ROWS + first: (4 * j + i) * ROWS + first + 4, :] for i in range(4)]
                csend[step, side, 16 * j: 16 * j + 16, :] = jnp.concatenate(pieces, 0).astype(BF16)

    def unpack(step):
        def rows(q, carry):
            base = pl.multiple_of(q * 16, 16)
            low = xrecv[step, 0, pl.ds(base, 16), :].astype(F32)
            high = xrecv[step, 1, pl.ds(base, 16), :].astype(F32)
            for i in range(4):
                spot = pl.multiple_of((q * 4 + i) * SPAN, 8)
                ext[pl.ds(spot + 4, 4), :] = low[4 * i: 4 * i + 4]
                ext[pl.ds(spot + 16, 4), :] = high[4 * i: 4 * i + 4]
            return carry

        lax.fori_loop(0, nv // 4, rows, 0)
        for j in range(groups // 2):
            a = precv[step, 0, 16 * j: 16 * j + 16, :].astype(F32)
            b = precv[step, 1, 16 * j: 16 * j + 16, :].astype(F32)
            for i in range(2):
                spot = (2 * j + i) * SPAN
                pext[spot + 8: spot + 16, :] = jnp.where(from_left, a[8 * i: 8 * i + 8], b[8 * i: 8 * i + 8])
        pick = from_left[0:4]
        for j in range(groups // 4):
            parts = [crecv[step, c, 16 * j: 16 * j + 16, :].astype(F32) for c in range(4)]
            for i in range(4):
                spot = (4 * j + i) * SPAN
                cut = slice(4 * i, 4 * i + 4)
                pext[spot + 4: spot + 8, :] = jnp.where(pick, parts[0][cut], parts[1][cut])
                pext[spot + 16: spot + 20, :] = jnp.where(pick, parts[2][cut], parts[3][cut])

    def speeds(v):
        return disp[0, v].astype(F32) + frac[0, v], disp[1, v].astype(F32) + frac[1, v]

    def source(main, side, shift):
        low, high = jnp.minimum(-shift, 0), jnp.maximum(-shift, 0)
        return jnp.where((centered >= low) & (centered < high), side, main)

    def turn(plane, shift):
        return pltpu.roll(plane, jnp.where(shift < 0, shift + LANES, shift), 1)

    def transport(g, k):
        v = g * GROUP + k
        mx, my = disp[0, v], disp[1, v]
        a, b = frac[0, v], frac[1, v]
        start = v * SPAN + 8 - mx
        main = (1.0 - a) * ext[pl.ds(start, ROWS), :] + a * ext[pl.ds(start - 1, ROWS), :]
        pstart = g * SPAN + 8 - mx
        side = (1.0 - a) * pext[pl.ds(pstart, ROWS), :] + a * pext[pl.ds(pstart - 1, ROWS), :]
        side = pltpu.roll(side, (2 * LANES - 8 * k - 4) % LANES, 1)
        near = turn(source(main, side, my), my)
        far = turn(source(main, side, my + 1), my + 1)
        return (1.0 - b) * near + b * far

    def add_over_vel(step, count, sref, rref, ssem, rsem, values):
        for i, value in enumerate(values):
            sref[step, i * ROWS: (i + 1) * ROWS, :] = value
        copies = [
            remote(sref.at[step], rref.at[step, p], ssem.at[step, p], rsem.at[step, p], at(peers[p], sx, sy))
            for p in range(nvel - 1)
        ]
        for copy in copies:
            copy.start()
        for copy in copies:
            copy.wait()
        totals = []
        for i, value in enumerate(values):
            for p in range(nvel - 1):
                value = value + rref[step, p, i * ROWS: (i + 1) * ROWS, :]
            totals.append(value)
        return totals

    zero = jnp.zeros((ROWS, LANES), F32)
    relax = 1.0 - jnp.exp(-freq_ref[...])
    solid = solid_ref[...] > 0
    wall_scale = -LOG2E / (2.0 * (zero + heat[0]))

    def load_group(g, carry):
        planes = []
        for k in range(0, GROUP, 2):
            pair = x_ref[pl.ds(pl.multiple_of(g * (GROUP * ROWS) + k * ROWS, 16), 16), :].astype(F32)
            planes += [pair[0:8], pair[8:16]]
        stow(0, g, planes)
        return carry

    lax.fori_loop(0, groups, load_group, 0)
    finish_pack(0)
    pl.semaphore_wait(barrier, len(spatial) + nvel - 1)

    wall_sum = None
    for step in range(STEPS):
        copies = halo_copies(step)
        for copy in copies:
            copy.start()
        if step == 0:
            def wall_group(g, total):
                for k in range(GROUP):
                    v = g * GROUP + k
                    cx, cy = speeds(v)
                    w = jnp.exp2((cx * cx + cy * cy) * wall_scale)
                    wall_ref[pl.ds(pl.multiple_of(v * ROWS, 8), ROWS), :] = w
                    total = total + w
                return total

            wall_sum = lax.fori_loop(0, groups, wall_group, zero)
        for copy in copies:
            copy.wait()
        unpack(step)

        def moment_group(g, carry):
            density, flux_x, flux_y, energy = carry
            for k in range(GROUP):
                v = g * GROUP + k
                cx, cy = speeds(v)
                moved = transport(g, k)
                moved_ref[pl.ds(pl.multiple_of(v * ROWS, 8), ROWS), :] = moved
                density = density + moved
                flux_x = flux_x + moved * cx
                flux_y = flux_y + moved * cy
                energy = energy + moved * (cx * cx + cy * cy)
            return density, flux_x, flux_y, energy

        moments = list(lax.fori_loop(0, groups, moment_group, (zero, zero, zero, zero)))
        extra = [wall_sum] if step == 0 else [zero]
        totals = add_over_vel(step, 5, msend, mrecv, ms_sem, mr_sem, moments + extra)
        density, flux_x, flux_y, energy = totals[:4]
        if step == 0:
            wall_sum = totals[4]
        drift_x = flux_x / density
        drift_y = flux_y / density
        thermal = 0.5 * (energy / density - drift_x * drift_x - drift_y * drift_y)
        scale = -LOG2E / (2.0 * thermal)

        def profile_group(g, total):
            for k in range(GROUP):
                v = g * GROUP + k
                cx, cy = speeds(v)
                off_x = cx - drift_x
                off_y = cy - drift_y
                value = jnp.exp2((off_x * off_x + off_y * off_y) * scale)
                prof_ref[pl.ds(pl.multiple_of(v * ROWS, 8), ROWS), :] = value
                total = total + value
            return total

        partition = lax.fori_loop(0, groups, profile_group, zero)
        (partition,) = add_over_vel(step, 1, zsend, zrecv, zs_sem, zr_sem, [partition])
        keep = 1.0 - relax
        gain = relax * density / partition
        wall_gain = density / wall_sum

        def relax_group(g, carry):
            planes = []
            for k in range(GROUP):
                rows = pl.ds(pl.multiple_of((g * GROUP + k) * ROWS, 8), ROWS)
                gas = keep * moved_ref[rows, :] + gain * prof_ref[rows, :]
                planes.append(jnp.where(solid, wall_gain * wall_ref[rows, :], gas))
            for k in range(0, GROUP, 2):
                pair = jnp.concatenate(planes[k: k + 2], 0).astype(BF16)
                if step == STEPS - 1:
                    o_ref[pl.ds(pl.multiple_of((g * GROUP + k) * ROWS, 16), 16), :] = pair
                else:
                    pair = pair.astype(F32)
                    planes[k: k + 2] = [pair[0:8], pair[8:16]]
            if step < STEPS - 1:
                stow(step + 1, g, planes)
            return carry

        lax.fori_loop(0, groups, relax_group, 0)
        if step < STEPS - 1:
            finish_pack(step + 1)


def per_device(sizes, particle_distributions, disp, frac, freq, solid, heat):
    nv, rows, lanes = particle_distributions.shape
    assert rows == ROWS and lanes == LANES and nv % (4 * GROUP) == 0
    nvel = sizes[0]
    others = max(nvel - 1, 1)
    groups = nv // GROUP
    dma = pltpu.SemaphoreType.DMA
    vmem = pl.BlockSpec(memory_space=pltpu.VMEM)
    smem = pl.BlockSpec(memory_space=pltpu.SMEM)
    out = pl.pallas_call(
        functools.partial(kernel, sizes),
        out_shape=jax.ShapeDtypeStruct((nv * ROWS, LANES), BF16),
        in_specs=[smem, smem, smem, vmem, vmem, vmem],
        out_specs=vmem,
        scratch_shapes=[
            pltpu.VMEM((nv * SPAN, LANES), F32),
            pltpu.VMEM((groups * SPAN, LANES), F32),
            pltpu.VMEM((groups * ROWS, LANES), F32),
            pltpu.VMEM((nv * ROWS, LANES), F32),
            pltpu.VMEM((nv * ROWS, LANES), F32),
            pltpu.VMEM((nv * ROWS, LANES), F32),
            pltpu.VMEM((STEPS, 2, nv * MAXS, LANES), BF16),
            pltpu.VMEM((STEPS, groups * ROWS, LANES), BF16),
            pltpu.VMEM((STEPS, 2, groups * MAXS, LANES), BF16),
            pltpu.VMEM((STEPS, 2, nv * MAXS, LANES), BF16),
            pltpu.VMEM((STEPS, 2, groups * ROWS, LANES), BF16),
            pltpu.VMEM((STEPS, 4, groups * MAXS, LANES), BF16),
            pltpu.VMEM((STEPS, 5 * ROWS, LANES), F32),
            pltpu.VMEM((STEPS, others, 5 * ROWS, LANES), F32),
            pltpu.VMEM((STEPS, ROWS, LANES), F32),
            pltpu.VMEM((STEPS, others, ROWS, LANES), F32),
            dma((STEPS, 2)), dma((STEPS, 2)),
            dma((STEPS, 2)), dma((STEPS, 2)),
            dma((STEPS, 4)), dma((STEPS, 4)),
            dma((STEPS, others)), dma((STEPS, others)),
            dma((STEPS, others)), dma((STEPS, others)),
        ],
        compiler_params=pltpu.CompilerParams(
            collective_id=0, has_side_effects=True, vmem_limit_bytes=40 << 20
        ),
        name="bgk",
    )(disp, frac, heat, particle_distributions.reshape(nv * ROWS, LANES), freq, solid)
    return out.reshape(nv, ROWS, LANES)


def solution(mesh):
    sizes = (mesh.shape["vel"], mesh.shape["sx"], mesh.shape["sy"])
    return jax.shard_map(
        functools.partial(per_device, sizes),
        mesh=mesh,
        in_specs=(
            P("vel", "sx", "sy"),
            P(None, "vel"),
            P(None, "vel"),
            P("sx", "sy"),
            P("sx", "sy"),
            P(),
        ),
        out_specs=P("vel", "sx", "sy"),
        check_vma=False,
    )
```

profile of v0, /device:TPU:0, one launch (start us, length us, event | category | flops | bytes accessed | tf_op | source)
XLA Modules:
  0.0 57.5 jit_solution(13647014398060503773)
XLA Ops:
  0.0 0.0 copy-start.3
  0.7 0.0 copy-done.3
  0.7 0.0 copy-start
  0.7 1.0 %copy-done = bf16[256,8,128]{2,1,0:T(8,128)(2,1)S(1)} copy-done((bf16[256,8,128]{2,1,0:T(8,128)(2,1)S(1)}, bf16[256,8,128]{2,1,0:T(8,128)(2,1)}, u32[]{:S(2)}) %copy-start) | copy-done | bytes 524312
  1.7 0.0 copy-start.1
  1.7 0.7 %copy-done.1 = f32[8,128]{1,0:T(8,128)S(1)} copy-done((f32[8,128]{1,0:T(8,128)S(1)}, f32[8,128]{1,0:T(8,128)}, u32[]{:S(2)}) %copy-start.1) | copy-done | bytes 4120
  2.4 0.0 copy-start.2
  2.4 0.7 %copy-done.2 = s32[8,128]{1,0:T(8,128)S(1)} copy-done((s32[8,128]{1,0:T(8,128)S(1)}, s32[8,128]{1,0:T(8,128)}, u32[]{:S(2)}) %copy-start.2) | copy-done | bytes 4120
  3.1 0.0 copy-start.4
  3.1 0.7 %copy-done.4 = f32[2,256]{1,0:T(2,128)S(1)} copy-done((f32[2,256]{1,0:T(2,128)S(1)}, f32[2,256]{1,0:T(2,128)}, u32[]{:S(2)}) %copy-start.4) | copy-done | bytes 2072
  3.8 52.9 %bgk.1 = bf16[2048,128]{1,0:T(8,128)(2,1)S(1)} custom-call(s32[2,256]{1,0:T(2,128)S(1)} %copy-done.3, f32[2,256]{1,0:T(2,128)S(1)} %copy-done.4, f32[1]{0:T(128)S(6)} %copy.8.heat, bf16[2048,128]{1,0:T(8,128)(2,1)S(1)} %bitcast.3, f32[8,128]{1,0:T(8,128)S(1)} %copy-done.1, s32[8,128]{1,0:T(8,128)S(1)} %copy-done.2), custom_call_target="tpu_custom_call" | custom-call | tf_op jit(solution)/shard_map/bgk/pallas_call | solution.py:301
  56.7 0.8 %copy.9 = bf16[256,8,128]{2,1,0:T(8,128)(2,1)} copy(bf16[256,8,128]{2,1,0:T(8,128)(2,1)S(1)} %bitcast.2) | data formatting | bytes 1048576
Async XLA Ops:
  0.0 0.7 %copy-start.3 = (s32[2,256]{1,0:T(2,128)S(1)}, s32[2,256]{1,0:T(2,128)}, u32[]{:S(2)}) copy-start(s32[2,256]{1,0:T(2,128)} %disp.1) | copy-start | bytes 6148
  0.7 1.0 %copy-start = (bf16[256,8,128]{2,1,0:T(8,128)(2,1)S(1)}, bf16[256,8,128]{2,1,0:T(8,128)(2,1)}, u32[]{:S(2)}) copy-start(bf16[256,8,128]{2,1,0:T(8,128)(2,1)} %param.6) | copy-start | bytes 1572868
  1.7 0.7 %copy-start.1 = (f32[8,128]{1,0:T(8,128)S(1)}, f32[8,128]{1,0:T(8,128)}, u32[]{:S(2)}) copy-start(f32[8,128]{1,0:T(8,128)} %freq_ref.1) | copy-start | bytes 12292
  2.4 0.7 %copy-start.2 = (s32[8,128]{1,0:T(8,128)S(1)}, s32[8,128]{1,0:T(8,128)}, u32[]{:S(2)}) copy-start(s32[8,128]{1,0:T(8,128)} %solid_ref.1) | copy-start | bytes 12292
  3.1 0.7 %copy-start.4 = (f32[2,256]{1,0:T(2,128)S(1)}, f32[2,256]{1,0:T(2,128)}, u32[]{:S(2)}) copy-start(f32[2,256]{1,0:T(2,128)} %frac.1) | copy-start | bytes 6148
where the time goes:
time: 57.7 us; the launch traced here: 57.5 us
  Pallas kernels  52.9 us (92%)
  local copies, waits for them, and re-layouts  3.9 us (7%)
  between operations  0.68 us (1%)
    pallas_call x1, Pallas kernels, per_device(): pl.pallas_call(functools.partial(kernel, sizes), out_shape=jax.ShapeDtype...  52.9 us
    unnamed x11, local copies, waits for them, and re-layouts  3.9 us

commit v1 on v0

--- a/solution.py
+++ b/solution.py
@@ -13,6 +13,8 @@
 ROWS = 8
 LANES = 128
 GROUP = 16
+PART = 4
+CHUNK = GROUP * PART
 SPAN = 24
 LOG2E = math.log2(math.e)
 F32 = jnp.float32
@@ -21,13 +23,19 @@
 
 def kernel(
     sizes,
+    heat,
+    disp_in,
+    frac_in,
+    x_in,
+    freq_in,
+    solid_in,
+    o_ref,
     disp,
     frac,
-    heat,
     x_ref,
     freq_ref,
     solid_ref,
-    o_ref,
+    in_sem,
     ext,
     pext,
     pack_f,
@@ -57,7 +65,15 @@
 ):
     nvel, nsx, nsy = sizes
     nv = disp.shape[1]
-    groups = nv // GROUP
+    chunks = nv // CHUNK
+    loads = [
+        pltpu.make_async_copy(src, dst, in_sem.at[i])
+        for i, (src, dst) in enumerate(
+            [(x_in, x_ref), (disp_in, disp), (frac_in, frac), (freq_in, freq_ref), (solid_in, solid_ref)]
+        )
+    ]
+    for load in loads:
+        load.start()
     vel = lax.axis_index("vel")
     sx = lax.axis_index("sx")
     sy = lax.axis_index("sy")
@@ -88,17 +104,26 @@
             device_id=target, device_id_type=pl.DeviceIdType.MESH,
         )
 
-    def halo_copies(step):
-        copies = [
-            remote(xsend.at[step, 0], xrecv.at[step, 0], xs_sem.at[step, 0], xr_sem.at[step, 0], spatial[0]),
-            remote(xsend.at[step, 1], xrecv.at[step, 1], xs_sem.at[step, 1], xr_sem.at[step, 1], spatial[1]),
-            remote(psend.at[step], precv.at[step, 0], ps_sem.at[step, 0], pr_sem.at[step, 0], spatial[2]),
-            remote(psend.at[step], precv.at[step, 1], ps_sem.at[step, 1], pr_sem.at[step, 1], spatial[3]),
-        ]
-        for c in range(4):
-            copies.append(
-                remote(csend.at[step, c // 2], crecv.at[step, c], cs_sem.at[step, c], cr_sem.at[step, c], spatial[4 + c])
-            )
+    def halo_copies(step, c):
+        rows = pl.ds(pl.multiple_of(c * (CHUNK * MAXS), 16), CHUNK * MAXS)
+        prows = pl.ds(pl.multiple_of(c * (PART * ROWS), 16), PART * ROWS)
+        crows = pl.ds(pl.multiple_of(c * (PART * MAXS), 16), PART * MAXS)
+        copies = []
+        for d in range(2):
+            copies.append(remote(
+                psend.at[step, prows], precv.at[step, d, prows],
+                ps_sem.at[step, c, d], pr_sem.at[step, c, d], spatial[2 + d],
+            ))
+        for d in range(4):
+            copies.append(remote(
+                csend.at[step, d // 2, crows], crecv.at[step, d, crows],
+                cs_sem.at[step, c, d], cr_sem.at[step, c, d], spatial[4 + d],
+            ))
+        for d in range(2):
+            copies.append(remote(
+                xsend.at[step, d, rows], xrecv.at[step, d, rows],
+                xs_sem.at[step, c, d], xr_sem.at[step, c, d], spatial[d],
+            ))
         return copies
 
     def stow(step, g, planes):
@@ -114,15 +139,27 @@
             xsend[step, 0, pl.ds(base, 16), :] = jnp.concatenate([f[4:8] for f in four], 0).astype(BF16)
             xsend[step, 1, pl.ds(base, 16), :] = jnp.concatenate([f[0:4] for f in four], 0).astype(BF16)
 
-    def finish_pack(step):
-        psend[step] = pack_f[...].astype(BF16)
-        for j in range(groups // 4):
-            for side, first in ((0, 4), (1, 0)):
-                pieces = [pack_f[(4 * j + i) * ROWS + first: (4 * j + i) * ROWS + first + 4, :] for i in range(4)]
-                csend[step, side, 16 * j: 16 * j + 16, :] = jnp.concatenate(pieces, 0).astype(BF16)
-
-    def unpack(step):
-        def rows(q, carry):
+    def send_chunk(step, c):
+        tops, bottoms, fulls = [], [], []
+        for i in range(PART):
+            plane = pack_f[pl.ds(pl.multiple_of((c * PART + i) * ROWS, 8), ROWS), :]
+            tops.append(plane[4:8])
+            bottoms.append(plane[0:4])
+            fulls.append(plane)
+        base = pl.multiple_of(c * (PART * MAXS), 16)
+        csend[step, 0, pl.ds(base, 16), :] = jnp.concatenate(tops, 0).astype(BF16)
+        csend[step, 1, pl.ds(base, 16), :] = jnp.concatenate(bottoms, 0).astype(BF16)
+        base = pl.multiple_of(c * (PART * ROWS), 16)
+        psend[step, pl.ds(base, PART * ROWS), :] = jnp.concatenate(fulls, 0).astype(BF16)
+        for copy in halo_copies(step, c):
+            copy.start()
+
+    def receive_chunk(step, c):
+        for copy in halo_copies(step, c):
+            copy.wait_recv()
+
+        def rows(i, carry):
+            q = c * (CHUNK // 4) + i
             base = pl.multiple_of(q * 16, 16)
             low = xrecv[step, 0, pl.ds(base, 16), :].astype(F32)
             high = xrecv[step, 1, pl.ds(base, 16), :].astype(F32)
@@ -132,21 +169,20 @@
                 ext[pl.ds(spot + 16, 4), :] = high[4 * i: 4 * i + 4]
             return carry
 
-        lax.fori_loop(0, nv // 4, rows, 0)
-        for j in range(groups // 2):
-            a = precv[step, 0, 16 * j: 16 * j + 16, :].astype(F32)
-            b = precv[step, 1, 16 * j: 16 * j + 16, :].astype(F32)
-            for i in range(2):
-                spot = (2 * j + i) * SPAN
-                pext[spot + 8: spot + 16, :] = jnp.where(from_left, a[8 * i: 8 * i + 8], b[8 * i: 8 * i + 8])
+        lax.fori_loop(0, CHUNK // 4, rows, 0, unroll=4)
+        base = pl.multiple_of(c * (PART * ROWS), 16)
+        a = precv[step, 0, pl.ds(base, PART * ROWS), :].astype(F32)
+        b = precv[step, 1, pl.ds(base, PART * ROWS), :].astype(F32)
+        base = pl.multiple_of(c * (PART * MAXS), 16)
+        corners = [crecv[step, d, pl.ds(base, 16), :].astype(F32) for d in range(4)]
         pick = from_left[0:4]
-        for j in range(groups // 4):
-            parts = [crecv[step, c, 16 * j: 16 * j + 16, :].astype(F32) for c in range(4)]
-            for i in range(4):
-                spot = (4 * j + i) * SPAN
-                cut = slice(4 * i, 4 * i + 4)
-                pext[spot + 4: spot + 8, :] = jnp.where(pick, parts[0][cut], parts[1][cut])
-                pext[spot + 16: spot + 20, :] = jnp.where(pick, parts[2][cut], parts[3][cut])
+        for i in range(PART):
+            spot = pl.multiple_of((c * PART + i) * SPAN, 8)
+            cut = slice(ROWS * i, ROWS * i + ROWS)
+            pext[pl.ds(spot + 8, ROWS), :] = jnp.where(from_left, a[cut], b[cut])
+            cut = slice(4 * i, 4 * i + 4)
+            pext[pl.ds(spot + 4, 4), :] = jnp.where(pick, corners[0][cut], corners[1][cut])
+            pext[pl.ds(spot + 16, 4), :] = jnp.where(pick, corners[2][cut], corners[3][cut])
 
     def speeds(v):
         return disp[0, v].astype(F32) + frac[0, v], disp[1, v].astype(F32) + frac[1, v]
@@ -189,7 +225,11 @@
             totals.append(value)
         return totals
 
+    groups = nv // GROUP
     zero = jnp.zeros((ROWS, LANES), F32)
+    for load in loads:
+        load.wait()
+    pl.semaphore_wait(barrier, len(spatial) + nvel - 1)
     relax = 1.0 - jnp.exp(-freq_ref[...])
     solid = solid_ref[...] > 0
     wall_scale = -LOG2E / (2.0 * (zero + heat[0]))
@@ -202,15 +242,15 @@
         stow(0, g, planes)
         return carry
 
-    lax.fori_loop(0, groups, load_group, 0)
-    finish_pack(0)
-    pl.semaphore_wait(barrier, len(spatial) + nvel - 1)
+    def load_chunk(c, carry):
+        lax.fori_loop(c * PART, (c + 1) * PART, load_group, 0)
+        send_chunk(0, c)
+        return carry
+
+    lax.fori_loop(0, chunks, load_chunk, 0)
 
     wall_sum = None
     for step in range(STEPS):
-        copies = halo_copies(step)
-        for copy in copies:
-            copy.start()
         if step == 0:
             def wall_group(g, total):
                 for k in range(GROUP):
@@ -222,9 +262,6 @@
                 return total
 
             wall_sum = lax.fori_loop(0, groups, wall_group, zero)
-        for copy in copies:
-            copy.wait()
-        unpack(step)
 
         def moment_group(g, carry):
             density, flux_x, flux_y, energy = carry
@@ -239,7 +276,11 @@
                 energy = energy + moved * (cx * cx + cy * cy)
             return density, flux_x, flux_y, energy
 
-        moments = list(lax.fori_loop(0, groups, moment_group, (zero, zero, zero, zero)))
+        def moment_chunk(c, carry):
+            receive_chunk(step, c)
+            return lax.fori_loop(c * PART, (c + 1) * PART, moment_group, carry)
+
+        moments = list(lax.fori_loop(0, chunks, moment_chunk, (zero, zero, zero, zero)))
         extra = [wall_sum] if step == 0 else [zero]
         totals = add_over_vel(step, 5, msend, mrecv, ms_sem, mr_sem, moments + extra)
         density, flux_x, flux_y, energy = totals[:4]
@@ -284,26 +325,46 @@
                 stow(step + 1, g, planes)
             return carry
 
-        lax.fori_loop(0, groups, relax_group, 0)
-        if step < STEPS - 1:
-            finish_pack(step + 1)
+        def relax_chunk(c, carry):
+            lax.fori_loop(c * PART, (c + 1) * PART, relax_group, 0)
+            if step < STEPS - 1:
+                send_chunk(step + 1, c)
+            return carry
+
+        lax.fori_loop(0, chunks, relax_chunk, 0)
+
+    def drain(c, carry):
+        for step in range(STEPS):
+            for copy in halo_copies(step, c):
+                copy.wait_send()
+        return carry
+
+    lax.fori_loop(0, chunks, drain, 0)
 
 
 def per_device(sizes, particle_distributions, disp, frac, freq, solid, heat):
     nv, rows, lanes = particle_distributions.shape
-    assert rows == ROWS and lanes == LANES and nv % (4 * GROUP) == 0
+    assert rows == ROWS and lanes == LANES and nv % CHUNK == 0
     nvel = sizes[0]
     others = max(nvel - 1, 1)
     groups = nv // GROUP
+    chunks = nv // CHUNK
     dma = pltpu.SemaphoreType.DMA
     vmem = pl.BlockSpec(memory_space=pltpu.VMEM)
+    hbm = pl.BlockSpec(memory_space=pltpu.MemorySpace.HBM)
     smem = pl.BlockSpec(memory_space=pltpu.SMEM)
     out = pl.pallas_call(
         functools.partial(kernel, sizes),
         out_shape=jax.ShapeDtypeStruct((nv * ROWS, LANES), BF16),
-        in_specs=[smem, smem, smem, vmem, vmem, vmem],
+        in_specs=[smem, hbm, hbm, hbm, hbm, hbm],
         out_specs=vmem,
         scratch_shapes=[
+            pltpu.SMEM((2, nv), jnp.int32),
+            pltpu.SMEM((2, nv), F32),
+            pltpu.VMEM((nv * ROWS, LANES), BF16),
+            pltpu.VMEM((ROWS, LANES), F32),
+            pltpu.VMEM((ROWS, LANES), jnp.int32),
+            dma((5,)),
             pltpu.VMEM((nv * SPAN, LANES), F32),
             pltpu.VMEM((groups * SPAN, LANES), F32),
             pltpu.VMEM((groups * ROWS, LANES), F32),
@@ -320,17 +381,17 @@
             pltpu.VMEM((STEPS, others, 5 * ROWS, LANES), F32),
             pltpu.VMEM((STEPS, ROWS, LANES), F32),
             pltpu.VMEM((STEPS, others, ROWS, LANES), F32),
-            dma((STEPS, 2)), dma((STEPS, 2)),
-            dma((STEPS, 2)), dma((STEPS, 2)),
-            dma((STEPS, 4)), dma((STEPS, 4)),
+            dma((STEPS, chunks, 2)), dma((STEPS, chunks, 2)),
+            dma((STEPS, chunks, 2)), dma((STEPS, chunks, 2)),
+            dma((STEPS, chunks, 4)), dma((STEPS, chunks, 4)),
             dma((STEPS, others)), dma((STEPS, others)),
             dma((STEPS, others)), dma((STEPS, others)),
         ],
         compiler_params=pltpu.CompilerParams(
-            collective_id=0, has_side_effects=True, vmem_limit_bytes=40 << 20
+            collective_id=0, has_side_effects=True, vmem_limit_bytes=63 << 20
         ),
         name="bgk",
-    )(disp, frac, heat, particle_distributions.reshape(nv * ROWS, LANES), freq, solid)
+    )(heat, disp, frac, particle_distributions.reshape(nv * ROWS, LANES), freq, solid)
     return out.reshape(nv, ROWS, LANES)
 
 

time: 57.7 us -> 49.4 us (0.86)
  Pallas kernels: 52.9 us -> 46.7 us
  local copies, waits for them, and re-layouts: 3.9 us -> 1.87 us
    pallas_call x1, Pallas kernels: 52.9 us -> 46.7 us  [per_device(): pl.pallas_call(functools.partial(kernel, sizes), out_shape=jax.ShapeDtype...]
    unnamed x11 -> x1, local copies, waits for them, and re-layouts: 3.9 us -> 1.87 us
where the time goes in v1:
time: 49.4 us; the launch traced here: 49.3 us
  Pallas kernels  46.7 us (95%)
  local copies, waits for them, and re-layouts  1.87 us (4%)
  between operations  0.66 us (1%)
    pallas_call x1, Pallas kernels, per_device(): pl.pallas_call(functools.partial(kernel, sizes), out_shape=jax.ShapeDtype...  46.7 us
    unnamed x1, local copies, waits for them, and re-layouts  1.87 us

profile of v1, /device:TPU:0, one launch (start us, length us, event | category | flops | bytes accessed | tf_op | source)
XLA Modules:
  0.0 49.3 jit_solution(9920891109384736939)
XLA Ops:
  0.7 46.7 %bgk.1 = bf16[2048,128]{1,0:T(8,128)(2,1)} custom-call(f32[1]{0:T(128)S(6)} %copy.8.heat, s32[2,256]{1,0:T(2,128)} %disp_in.1, f32[2,256]{1,0:T(2,128)} %frac_in.1, bf16[2048,128]{1,0:T(8,128)(2,1)} %bitcast.3, f32[8,128]{1,0:T(8,128)} %freq_in.1, s32[8,128]{1,0:T(8,128)} %solid_in.1), custom_call_target="tpu_custom_call" | custom-call | tf_op jit(solution)/shard_map/bgk/pallas_call | solution.py:356
  47.4 1.9 %copy.9 = bf16[256,8,128]{2,1,0:T(8,128)(2,1)} copy(bf16[256,8,128]{2,1,0:T(8,128)(2,1)} %bitcast.2) | data formatting | bytes 1048576

commit v2 on v1

--- a/solution.py
+++ b/solution.py
@@ -23,6 +23,7 @@
 
 def kernel(
     sizes,
+    general,
     heat,
     disp_in,
     frac_in,
@@ -30,6 +31,7 @@
     freq_in,
     solid_in,
     o_ref,
+    flag_ref,
     disp,
     frac,
     x_ref,
@@ -104,8 +106,12 @@
             device_id=target, device_id_type=pl.DeviceIdType.MESH,
         )
 
-    def halo_copies(step, c):
-        rows = pl.ds(pl.multiple_of(c * (CHUNK * MAXS), 16), CHUNK * MAXS)
+    def reach(c):
+        part = (vel * chunks + c) * (2 * MAXS) // (nvel * chunks)
+        upward = jnp.where(part >= MAXS, jnp.minimum(part - MAXS + 2, MAXS), jnp.where(part == MAXS - 1, 1, 0))
+        return upward, jnp.maximum(MAXS - part, 0)
+
+    def lane_copies(step, c):
         prows = pl.ds(pl.multiple_of(c * (PART * ROWS), 16), PART * ROWS)
         crows = pl.ds(pl.multiple_of(c * (PART * MAXS), 16), PART * MAXS)
         copies = []
@@ -119,12 +125,23 @@
                 csend.at[step, d // 2, crows], crecv.at[step, d, crows],
                 cs_sem.at[step, c, d], cr_sem.at[step, c, d], spatial[4 + d],
             ))
+        return copies
+
+    def row_copy(step, c, d, j):
+        rows = pl.ds(pl.multiple_of(c * CHUNK, 16), CHUNK)
+        return remote(
+            xsend.at[step, d, j, rows], xrecv.at[step, d, j, rows],
+            xs_sem.at[step, c, d, j], xr_sem.at[step, c, d, j], spatial[d],
+        )
+
+    def each_row(c, body):
+        limits = reach(c)
         for d in range(2):
-            copies.append(remote(
-                xsend.at[step, d, rows], xrecv.at[step, d, rows],
-                xs_sem.at[step, c, d], xr_sem.at[step, c, d], spatial[d],
-            ))
-        return copies
+            for j in range(MAXS):
+                if general:
+                    body(d, j)
+                else:
+                    pl.when(j < limits[d])(functools.partial(body, d, j))
 
     def stow(step, g, planes):
         packed = None
@@ -133,11 +150,6 @@
             turned = pltpu.roll(plane, (8 * k + 4) % LANES, 1)
             packed = turned if packed is None else jnp.where(slot == k, turned, packed)
         pack_f[pl.ds(pl.multiple_of(g * ROWS, 8), ROWS), :] = packed
-        for q in range(GROUP // 4):
-            four = planes[4 * q: 4 * q + 4]
-            base = pl.multiple_of(g * (GROUP * 4) + q * 16, 16)
-            xsend[step, 0, pl.ds(base, 16), :] = jnp.concatenate([f[4:8] for f in four], 0).astype(BF16)
-            xsend[step, 1, pl.ds(base, 16), :] = jnp.concatenate([f[0:4] for f in four], 0).astype(BF16)
 
     def send_chunk(step, c):
         tops, bottoms, fulls = [], [], []
@@ -151,25 +163,35 @@
         csend[step, 1, pl.ds(base, 16), :] = jnp.concatenate(bottoms, 0).astype(BF16)
         base = pl.multiple_of(c * (PART * ROWS), 16)
         psend[step, pl.ds(base, PART * ROWS), :] = jnp.concatenate(fulls, 0).astype(BF16)
-        for copy in halo_copies(step, c):
+        for copy in lane_copies(step, c):
             copy.start()
 
+        def send_row(d, j):
+            row = ROWS + (ROWS - 1 - j if d == 0 else j)
+            for i in range(CHUNK // 16):
+                first = pl.multiple_of(c * (CHUNK * SPAN), 8) + i * (16 * SPAN) + row
+                halves = [ext[pl.ds(first + h * (8 * SPAN), 8, stride=SPAN), :] for h in range(2)]
+                spot = pl.multiple_of(c * CHUNK + i * 16, 16)
+                xsend[step, d, j, pl.ds(spot, 16), :] = jnp.concatenate(halves, 0).astype(BF16)
+            row_copy(step, c, d, j).start()
+
+        each_row(c, send_row)
+
     def receive_chunk(step, c):
-        for copy in halo_copies(step, c):
+        for copy in lane_copies(step, c):
             copy.wait_recv()
 
-        def rows(i, carry):
-            q = c * (CHUNK // 4) + i
-            base = pl.multiple_of(q * 16, 16)
-            low = xrecv[step, 0, pl.ds(base, 16), :].astype(F32)
-            high = xrecv[step, 1, pl.ds(base, 16), :].astype(F32)
-            for i in range(4):
-                spot = pl.multiple_of((q * 4 + i) * SPAN, 8)
-                ext[pl.ds(spot + 4, 4), :] = low[4 * i: 4 * i + 4]
-                ext[pl.ds(spot + 16, 4), :] = high[4 * i: 4 * i + 4]
-            return carry
-
-        lax.fori_loop(0, CHUNK // 4, rows, 0, unroll=4)
+        def receive_row(d, j):
+            row_copy(step, c, d, j).wait_recv()
+            row = ROWS - 1 - j if d == 0 else 2 * ROWS + j
+            for i in range(CHUNK // 16):
+                spot = pl.multiple_of(c * CHUNK + i * 16, 16)
+                pair = xrecv[step, d, j, pl.ds(spot, 16), :].astype(F32)
+                first = pl.multiple_of(c * (CHUNK * SPAN), 8) + i * (16 * SPAN) + row
+                for h in range(2):
+                    ext[pl.ds(first + h * (8 * SPAN), 8, stride=SPAN), :] = pair[8 * h: 8 * h + 8]
+
+        each_row(c, receive_row)
         base = pl.multiple_of(c * (PART * ROWS), 16)
         a = precv[step, 0, pl.ds(base, PART * ROWS), :].astype(F32)
         b = precv[step, 1, pl.ds(base, PART * ROWS), :].astype(F32)
@@ -252,16 +274,19 @@
     wall_sum = None
     for step in range(STEPS):
         if step == 0:
-            def wall_group(g, total):
+            def wall_group(g, carry):
+                total, beyond = carry
+                upward, downward = reach(g // PART)
                 for k in range(GROUP):
                     v = g * GROUP + k
+                    beyond = jnp.maximum(beyond, jnp.where(disp[0, v] < 0, -disp[0, v] - downward, disp[0, v] + 1 - upward))
                     cx, cy = speeds(v)
                     w = jnp.exp2((cx * cx + cy * cy) * wall_scale)
                     wall_ref[pl.ds(pl.multiple_of(v * ROWS, 8), ROWS), :] = w
                     total = total + w
-                return total
-
-            wall_sum = lax.fori_loop(0, groups, wall_group, zero)
+                return total, beyond
+
+            wall_sum, beyond = lax.fori_loop(0, groups, wall_group, (zero, jnp.int32(0)))
 
         def moment_group(g, carry):
             density, flux_x, flux_y, energy = carry
@@ -281,11 +306,12 @@
             return lax.fori_loop(c * PART, (c + 1) * PART, moment_group, carry)
 
         moments = list(lax.fori_loop(0, chunks, moment_chunk, (zero, zero, zero, zero)))
-        extra = [wall_sum] if step == 0 else [zero]
-        totals = add_over_vel(step, 5, msend, mrecv, ms_sem, mr_sem, moments + extra)
+        extra = [wall_sum, zero + beyond.astype(F32)] if step == 0 else [zero, zero]
+        totals = add_over_vel(step, 6, msend, mrecv, ms_sem, mr_sem, moments + extra)
         density, flux_x, flux_y, energy = totals[:4]
         if step == 0:
             wall_sum = totals[4]
+            flag_ref[...] = totals[5]
         drift_x = flux_x / density
         drift_y = flux_y / density
         thermal = 0.5 * (energy / density - drift_x * drift_x - drift_y * drift_y)
@@ -335,8 +361,9 @@
 
     def drain(c, carry):
         for step in range(STEPS):
-            for copy in halo_copies(step, c):
+            for copy in lane_copies(step, c):
                 copy.wait_send()
+            each_row(c, lambda d, j: row_copy(step, c, d, j).wait_send())
         return carry
 
     lax.fori_loop(0, chunks, drain, 0)
@@ -353,11 +380,15 @@
     vmem = pl.BlockSpec(memory_space=pltpu.VMEM)
     hbm = pl.BlockSpec(memory_space=pltpu.MemorySpace.HBM)
     smem = pl.BlockSpec(memory_space=pltpu.SMEM)
-    out = pl.pallas_call(
-        functools.partial(kernel, sizes),
-        out_shape=jax.ShapeDtypeStruct((nv * ROWS, LANES), BF16),
+    def call(general):
+        return pl.pallas_call(
+        functools.partial(kernel, sizes, general),
+        out_shape=(
+            jax.ShapeDtypeStruct((nv * ROWS, LANES), BF16),
+            jax.ShapeDtypeStruct((ROWS, LANES), F32),
+        ),
         in_specs=[smem, hbm, hbm, hbm, hbm, hbm],
-        out_specs=vmem,
+        out_specs=(vmem, vmem),
         scratch_shapes=[
             pltpu.SMEM((2, nv), jnp.int32),
             pltpu.SMEM((2, nv), F32),
@@ -371,27 +402,31 @@
             pltpu.VMEM((nv * ROWS, LANES), F32),
             pltpu.VMEM((nv * ROWS, LANES), F32),
             pltpu.VMEM((nv * ROWS, LANES), F32),
-            pltpu.VMEM((STEPS, 2, nv * MAXS, LANES), BF16),
+            pltpu.VMEM((STEPS, 2, MAXS, nv, LANES), BF16),
             pltpu.VMEM((STEPS, groups * ROWS, LANES), BF16),
             pltpu.VMEM((STEPS, 2, groups * MAXS, LANES), BF16),
-            pltpu.VMEM((STEPS, 2, nv * MAXS, LANES), BF16),
+            pltpu.VMEM((STEPS, 2, MAXS, nv, LANES), BF16),
             pltpu.VMEM((STEPS, 2, groups * ROWS, LANES), BF16),
             pltpu.VMEM((STEPS, 4, groups * MAXS, LANES), BF16),
-            pltpu.VMEM((STEPS, 5 * ROWS, LANES), F32),
-            pltpu.VMEM((STEPS, others, 5 * ROWS, LANES), F32),
+            pltpu.VMEM((STEPS, 6 * ROWS, LANES), F32),
+            pltpu.VMEM((STEPS, others, 6 * ROWS, LANES), F32),
             pltpu.VMEM((STEPS, ROWS, LANES), F32),
             pltpu.VMEM((STEPS, others, ROWS, LANES), F32),
-            dma((STEPS, chunks, 2)), dma((STEPS, chunks, 2)),
+            dma((STEPS, chunks, 2, MAXS)), dma((STEPS, chunks, 2, MAXS)),
             dma((STEPS, chunks, 2)), dma((STEPS, chunks, 2)),
             dma((STEPS, chunks, 4)), dma((STEPS, chunks, 4)),
             dma((STEPS, others)), dma((STEPS, others)),
             dma((STEPS, others)), dma((STEPS, others)),
         ],
         compiler_params=pltpu.CompilerParams(
-            collective_id=0, has_side_effects=True, vmem_limit_bytes=63 << 20
+            collective_id=int(general), has_side_effects=True, vmem_limit_bytes=63 << 20
         ),
-        name="bgk",
-    )(heat, disp, frac, particle_distributions.reshape(nv * ROWS, LANES), freq, solid)
+        name="bgk_general" if general else "bgk",
+    )(*operands)
+
+    operands = (heat, disp, frac, particle_distributions.reshape(nv * ROWS, LANES), freq, solid)
+    out, flag = call(False)
+    out = lax.cond(flag[0, 0] > 0.0, lambda: call(True)[0], lambda: out)
     return out.reshape(nv, ROWS, LANES)
 
 

time: 49.4 us -> 40.6 us (0.82)
  Pallas kernels: 46.7 us -> 35.8 us
  local copies, waits for them, and re-layouts: 1.87 us -> 3.1 us
  between operations: 0.66 us -> 1.45 us
    pallas_call x1, Pallas kernels: 46.7 us -> 35.8 us  [call(): pl.pallas_call(functools.partial(kernel, sizes, general), out_shape=(jax....]
    slice x0 -> x1, local copies, waits for them, and re-layouts: none -> 1.2 us  [per_device(): out = lax.cond(flag[0, 0] > 0.0, lambda: call(True)[0], lambda: out)]
    unnamed x1 -> x11, local copies, waits for them, and re-layouts: 1.87 us -> 1.89 us
where the time goes in v2:
time: 40.6 us; the launch traced here: 40.4 us
  Pallas kernels  35.8 us (88%)
  local copies, waits for them, and re-layouts  3.1 us (8%)
  between operations  1.45 us (4%)
    pallas_call x1, Pallas kernels, call(): pl.pallas_call(functools.partial(kernel, sizes, general), out_shape=(jax....  35.8 us
    unnamed x11, local copies, waits for them, and re-layouts  1.89 us
    slice x1, local copies, waits for them, and re-layouts, per_device(): out = lax.cond(flag[0, 0] > 0.0, lambda: call(True)[0], lambda: out)  1.2 us

profile of v2, /device:TPU:0, one launch (start us, length us, event | category | flops | bytes accessed | tf_op | source)
XLA Modules:
  0.0 40.4 jit_solution(17207451844099452288)
XLA Ops:
  0.0 0.0 copy-start.1
  0.0 0.0 copy-start
  0.7 0.0 copy-done.1
  0.7 35.8 %bgk.1 = (bf16[2048,128]{1,0:T(8,128)(2,1)}, f32[8,128]{1,0:T(8,128)}) custom-call(f32[1]{0:T(128)S(6)} %copy.13.heat, s32[2,256]{1,0:T(2,128)} %disp_in.1, f32[2,256]{1,0:T(2,128)} %frac_in.1, bf16[2048,128]{1,0:T(8,128)(2,1)} %bitcast.4, f32[8,128]{1,0:T(8,128)S(1)} %copy-done.1, s32[8,128]{1,0:T(8,128)} %solid_in.1), custom_call_target="tpu_custom_call" | custom-call | tf_op jit(solution)/shard_map/bgk/pallas_call | solution.py:384
  36.5 0.0 copy-start.4
  36.6 0.0 copy-start.2
  36.6 1.2 %slice.3 = f32[1,1]{1,0:T(1,128)} slice(f32[8,128]{1,0:T(8,128)} %get-tuple-element.32), slice={[0:1], [0:1]} | slice | bytes 8 | tf_op jit(solution)/shard_map/slice | solution.py:429
  37.8 0.0 copy-start.3
  38.4 0.0 copy-done
  38.5 0.0 copy-done.4
  38.5 0.0 copy-done.2
  38.5 0.0 copy-done.3
  38.5 1.9 %copy.14 = bf16[256,8,128]{2,1,0:T(8,128)(2,1)} copy(bf16[256,8,128]{2,1,0:T(8,128)(2,1)} %get-tuple-element.34) | data formatting | bytes 1048576
  (1 shorter events, 0.0 us)
Async XLA Ops:
  0.0 0.7 %copy-start.1 = (f32[8,128]{1,0:T(8,128)S(1)}, f32[8,128]{1,0:T(8,128)}, u32[]{:S(2)}) copy-start(f32[8,128]{1,0:T(8,128)} %freq_in.1) | copy-start | bytes 12292
  0.0 38.4 %copy-start = (bf16[256,8,128]{2,1,0:T(8,128)(2,1)S(1)}, bf16[256,8,128]{2,1,0:T(8,128)(2,1)}, u32[]{:S(2)}) copy-start(bf16[256,8,128]{2,1,0:T(8,128)(2,1)} %param.8) | copy-start | bytes 1572868
  36.5 1.9 %copy-start.4 = (f32[2,256]{1,0:T(2,128)S(1)}, f32[2,256]{1,0:T(2,128)}, u32[]{:S(2)}) copy-start(f32[2,256]{1,0:T(2,128)} %frac_in.1) | copy-start | bytes 6148
  36.6 1.9 %copy-start.2 = (s32[8,128]{1,0:T(8,128)S(1)}, s32[8,128]{1,0:T(8,128)}, u32[]{:S(2)}) copy-start(s32[8,128]{1,0:T(8,128)} %solid_in.1) | copy-start | bytes 12292
  37.8 0.7 %copy-start.3 = (s32[2,256]{1,0:T(2,128)S(1)}, s32[2,256]{1,0:T(2,128)}, u32[]{:S(2)}) copy-start(s32[2,256]{1,0:T(2,128)} %disp_in.1) | copy-start | bytes 6148

commit v3 on v2

--- a/solution.py
+++ b/solution.py
@@ -30,8 +30,10 @@
     x_in,
     freq_in,
     solid_in,
+    o_hbm,
+    flag_ref,
     o_ref,
-    flag_ref,
+    out_sem,
     disp,
     frac,
     x_ref,
@@ -111,6 +113,10 @@
         upward = jnp.where(part >= MAXS, jnp.minimum(part - MAXS + 2, MAXS), jnp.where(part == MAXS - 1, 1, 0))
         return upward, jnp.maximum(MAXS - part, 0)
 
+    def out_copy(c):
+        rows = pl.ds(pl.multiple_of(c * (CHUNK * ROWS), 16), CHUNK * ROWS)
+        return pltpu.make_async_copy(o_ref.at[rows], o_hbm.at[rows], out_sem.at[c])
+
     def lane_copies(step, c):
         prows = pl.ds(pl.multiple_of(c * (PART * ROWS), 16), PART * ROWS)
         crows = pl.ds(pl.multiple_of(c * (PART * MAXS), 16), PART * MAXS)
@@ -311,7 +317,7 @@
         density, flux_x, flux_y, energy = totals[:4]
         if step == 0:
             wall_sum = totals[4]
-            flag_ref[...] = totals[5]
+            flag_ref[...] = totals[5][0:1, 0:1]
         drift_x = flux_x / density
         drift_y = flux_y / density
         thermal = 0.5 * (energy / density - drift_x * drift_x - drift_y * drift_y)
@@ -355,11 +361,14 @@
             lax.fori_loop(c * PART, (c + 1) * PART, relax_group, 0)
             if step < STEPS - 1:
                 send_chunk(step + 1, c)
+            else:
+                out_copy(c).start()
             return carry
 
         lax.fori_loop(0, chunks, relax_chunk, 0)
 
     def drain(c, carry):
+        out_copy(c).wait()
         for step in range(STEPS):
             for copy in lane_copies(step, c):
                 copy.wait_send()
@@ -385,11 +394,13 @@
         functools.partial(kernel, sizes, general),
         out_shape=(
             jax.ShapeDtypeStruct((nv * ROWS, LANES), BF16),
-            jax.ShapeDtypeStruct((ROWS, LANES), F32),
+            jax.ShapeDtypeStruct((1, 1), F32),
         ),
         in_specs=[smem, hbm, hbm, hbm, hbm, hbm],
-        out_specs=(vmem, vmem),
+        out_specs=(hbm, vmem),
         scratch_shapes=[
+            pltpu.VMEM((nv * ROWS, LANES), BF16),
+            dma((chunks,)),
             pltpu.SMEM((2, nv), jnp.int32),
             pltpu.SMEM((2, nv), F32),
             pltpu.VMEM((nv * ROWS, LANES), BF16),
@@ -426,7 +437,7 @@
 
     operands = (heat, disp, frac, particle_distributions.reshape(nv * ROWS, LANES), freq, solid)
     out, flag = call(False)
-    out = lax.cond(flag[0, 0] > 0.0, lambda: call(True)[0], lambda: out)
+    out = lax.cond(flag.reshape(()) > 0.0, lambda: call(True)[0], lambda: out)
     return out.reshape(nv, ROWS, LANES)
 
 

time: 40.6 us -> 40.3 us (level)
  local copies, waits for them, and re-layouts: 3.1 us -> 2.54 us
    slice x1 -> x0, local copies, waits for them, and re-layouts: 1.2 us -> none  [per_device(): out = lax.cond(flag[0, 0] > 0.0, lambda: call(True)[0], lambda: out)]
    unnamed x11, local copies, waits for them, and re-layouts: 1.89 us -> 2.54 us
where the time goes in v3:
time: 40.3 us; the launch traced here: 40 us
  Pallas kernels  36.1 us (90%)
  local copies, waits for them, and re-layouts  2.54 us (6%)
  between operations  1.4 us (3%)
    pallas_call x1, Pallas kernels, call(): pl.pallas_call(functools.partial(kernel, sizes, general), out_shape=(jax....  36.1 us
    unnamed x11, local copies, waits for them, and re-layouts  2.54 us

profile of v3, /device:TPU:0, one launch (start us, length us, event | category | flops | bytes accessed | tf_op | source)
XLA Modules:
  0.0 40.0 jit_solution(5388886046373580690)
XLA Ops:
  0.0 0.0 copy-start.1
  0.0 0.0 copy-start
  0.7 0.0 copy-done.1
  0.7 0.0 copy-start.4
  0.7 36.1 %bgk.1 = (bf16[2048,128]{1,0:T(8,128)(2,1)}, f32[1,1]{1,0:T(1,128)}) custom-call(f32[1]{0:T(128)S(6)} %copy.13.heat, s32[2,256]{1,0:T(2,128)} %disp_in.1, f32[2,256]{1,0:T(2,128)} %frac_in.1, bf16[2048,128]{1,0:T(8,128)(2,1)} %bitcast.4, f32[8,128]{1,0:T(8,128)S(1)} %copy-done.1, s32[8,128]{1,0:T(8,128)} %solid_in.1), custom_call_target="tpu_custom_call" | custom-call | tf_op jit(solution)/shard_map/bgk/pallas_call | solution.py:393
  36.8 0.0 copy-start.2
  37.5 0.0 copy-start.3
  37.5 0.0 copy-done
  37.5 0.0 copy-done.4
  37.5 0.0 copy-done.2
  37.5 0.6 %copy-done.3 = s32[2,256]{1,0:T(2,128)S(1)} copy-done((s32[2,256]{1,0:T(2,128)S(1)}, s32[2,256]{1,0:T(2,128)}, u32[]{:S(2)}) %copy-start.3) | copy-done | bytes 2072
  38.2 1.9 %copy.14 = bf16[256,8,128]{2,1,0:T(8,128)(2,1)} copy(bf16[256,8,128]{2,1,0:T(8,128)(2,1)} %get-tuple-element.34) | data formatting | bytes 1048576
  (1 shorter events, 0.0 us)
Async XLA Ops:
  0.0 0.7 %copy-start.1 = (f32[8,128]{1,0:T(8,128)S(1)}, f32[8,128]{1,0:T(8,128)}, u32[]{:S(2)}) copy-start(f32[8,128]{1,0:T(8,128)} %freq_in.1) | copy-start | bytes 12292
  0.0 37.5 %copy-start = (bf16[256,8,128]{2,1,0:T(8,128)(2,1)S(1)}, bf16[256,8,128]{2,1,0:T(8,128)(2,1)}, u32[]{:S(2)}) copy-start(bf16[256,8,128]{2,1,0:T(8,128)(2,1)} %param.8) | copy-start | bytes 1572868
  0.7 36.8 %copy-start.4 = (f32[2,256]{1,0:T(2,128)S(1)}, f32[2,256]{1,0:T(2,128)}, u32[]{:S(2)}) copy-start(f32[2,256]{1,0:T(2,128)} %frac_in.1) | copy-start | bytes 6148
  36.8 0.7 %copy-start.2 = (s32[8,128]{1,0:T(8,128)S(1)}, s32[8,128]{1,0:T(8,128)}, u32[]{:S(2)}) copy-start(s32[8,128]{1,0:T(8,128)} %solid_in.1) | copy-start | bytes 12292
  37.5 0.7 %copy-start.3 = (s32[2,256]{1,0:T(2,128)S(1)}, s32[2,256]{1,0:T(2,128)}, u32[]{:S(2)}) copy-start(s32[2,256]{1,0:T(2,128)} %disp_in.1) | copy-start | bytes 6148
